TPU v7x, 32 devices: a whole 2x2x4 slice. The times are simulated.
32 devices in a mesh: gx: 4 (over z), gy: 8 (over y, x, core).
Axes of the slice: x: 2, y: 2, z: 4, core: 2. Of those that a mesh axis runs over, the one named last changes fastest.
Arguments:
- right_side: float32 [2048, 4096], P('gx', 'gy'), may hold values from -8 to 8
- drift_x: float32 [2048, 4096], P('gx', 'gy'), may hold values from -0.9 to 0.9
- drift_y: float32 [2048, 4096], P('gx', 'gy'), may hold values from -0.9 to 0.9
- sketch_rows: float32 [256, 2048], P(None, 'gx'), may hold values from -0.375 to 0.375
- sketch_cols: float32 [256, 4096], P(None, 'gy'), may hold values from -6 to 6
Outputs:
- solution: float32 [2048, 4096], P('gx', 'gy')
- residual: float32 [2048, 4096], P('gx', 'gy')
All inputs are finite; a program needn't handle non-finite values.
Results may differ from a plain program's by a relative error of at most 0.0003.
Values sent between devices are 32-bit elements; how exact they have to be, the bound alone decides.
A program may use at most 64 MiB of HBM per device.

v0:
```python
import jax
import jax.numpy as jnp
from jax import lax
from jax.sharding import PartitionSpec as P

ITERS = 4
shift_value = 0.05


def padded_2(cells, sides, width):
    for axis, dim in sides:
        count = lax.axis_size(axis)
        ends = count - 1
        head = lax.slice_in_dim(cells, 0, width, axis=dim)
        tail = lax.slice_in_dim(cells, cells.shape[dim] - width, cells.shape[dim], axis=dim)
        cells = jnp.concatenate(
            [
                lax.ppermute(tail, axis, [(i, (i + 1) % count) for i in range(ends)]),
                cells,
                lax.ppermute(head, axis, [((i + 1) % count, i) for i in range(ends)]),
            ],
            axis=dim,
        )
    return cells


def stencil(padded, field, drift_x, drift_y):
    upper_cells = padded[:-2, 1:-1]
    lower_cells = padded[2:, 1:-1]
    left_cells = padded[1:-1, :-2]
    right_cells = padded[1:-1, 2:]
    return (
        (4.0 + shift_value) * field
        - (1.0 + drift_x) * upper_cells
        - (1.0 - drift_x) * lower_cells
        - (1.0 + drift_y) * left_cells
        - (1.0 - drift_y) * right_cells
    )


def solve_small(hessenberg, beta_norm):
    gram_matrix = jnp.dot(hessenberg.T, hessenberg, precision=lax.Precision.HIGHEST)
    target = beta_norm * hessenberg[0]
    factor = jnp.linalg.cholesky(gram_matrix)
    count = hessenberg.shape[1]
    forward = []
    for row in range(count):
        acc = target[row]
        for col in range(row):
            acc = acc - factor[row, col] * forward[col]
        forward.append(acc / factor[row, row])
    backward = [None] * count
    for row in reversed(range(count)):
        acc = forward[row]
        for col in range(row + 1, count):
            acc = acc - factor[col, row] * backward[col]
        backward[row] = acc / factor[row, row]
    return backward


def body(right_side, drift_x, drift_y, sketch_rows, sketch_cols):

    def sketch(field):
        product = jnp.dot(field, sketch_cols.T, precision=lax.Precision.HIGHEST)
        partial_value = jnp.einsum(
            "ki,ik->k", sketch_rows, product, precision=lax.Precision.HIGHEST
        )
        return lax.psum(partial_value, ("gx", "gy"))

    first_sketch = sketch(right_side)
    beta_norm = jnp.sqrt(jnp.sum(first_sketch * first_sketch))
    basis_vectors = [right_side / beta_norm]
    sketched = [first_sketch / beta_norm]
    images = []
    columns = []
    for column in range(ITERS):
        current = basis_vectors[column]
        padded = padded_2(current, (("gx", 0), ("gy", 1)), 1)
        applied = stencil(padded, current, drift_x, drift_y)
        images.append(applied)
        sketch_image = sketch(applied)
        sketch_matrix = jnp.stack(sketched, axis=1)
        projection = jnp.dot(sketch_matrix.T, sketch_image, precision=lax.Precision.HIGHEST)
        remainder = applied
        for index_prev in range(column + 1):
            remainder = remainder - projection[index_prev] * basis_vectors[index_prev]
        remainder_sketch = sketch_image - jnp.dot(
            sketch_matrix, projection, precision=lax.Precision.HIGHEST
        )
        new_norm = jnp.sqrt(jnp.sum(remainder_sketch * remainder_sketch))
        basis_vectors.append(remainder / new_norm)
        sketched.append(remainder_sketch / new_norm)
        entries = jnp.concatenate(
            [projection, new_norm[None], jnp.zeros((ITERS - column - 1,), jnp.float32)]
        )
        columns.append(entries)
    hessenberg = jnp.stack(columns, axis=1)
    coeffs = solve_small(hessenberg, beta_norm)
    solution = jnp.zeros_like(right_side)
    for column in range(ITERS):
        solution = solution + coeffs[column] * basis_vectors[column]
    padded = padded_2(solution, (("gx", 0), ("gy", 1)), 1)
    residual = right_side - stencil(padded, solution, drift_x, drift_y)
    return (solution, residual)


def solution(mesh):
    in_specs = (P("gx", "gy"), P("gx", "gy"), P("gx", "gy"), P(None, "gx"), P(None, "gy"))
    out_specs = (P("gx", "gy"), P("gx", "gy"))
    return jax.shard_map(body, mesh=mesh, in_specs=in_specs, out_specs=out_specs, check_vma=False)
```

profile of v0, /device:TPU:1, one launch (start us, length us, event | category | flops | bytes accessed | tf_op | source)
XLA Modules:
  0.0 370.7 jit_solution(15757160799951034432)
XLA Ops:
  4.3 40.5 %psum.35 = f32[256]{0:T(256)S(1)} all-reduce(f32[256]{0:T(256)S(1)} %multiply_reduce_fusion.4), channel_id=1, replica_groups=mesh['gx'=4,'gy'=8] {'gx','gy'}, use_global_device_ids=true, to_apply=%region_0.0 | all-reduce | flops 256 | bytes 2048 | tf_op jit(solution)/shard_map/psum | solution.py:68
  46.3 3.3 collective-permute-start
  50.9 3.0 collective-permute-done.1
  54.1 6.7 %collective-permute-start.2 = (f32[514,1]{1,0:T(8,128)S(1)}, f32[514,1]{1,0:T(8,128)S(1)}, u32[]{:S(2)}, u32[]{:S(2)}) collective-permute-start(f32[514,1]{1,0:T(8,128)S(1)} %get-tuple-element.16), channel_id=1, source_target_pairs={{0,1},{1,2},{2,3},{3,4},{4,5},{5,6},{6,7},{8,9},{9,10},{10,11},{11... | collective-permute-start | bytes 6176 | tf_op jit(solution)/shard_map/ppermute | solution.py:18
  64.1 4.5 %collective-permute-done.3 = f32[514,1]{1,0:T(8,128)S(1)} collective-permute-done((f32[514,1]{1,0:T(8,128)S(1)}, f32[514,1]{1,0:T(8,128)S(1)}, u32[]{:S(2)}, u32[]{:S(2)}) %collective-permute-start.3) | collective-permute-done | bytes 2088 | tf_op jit(solution)/shard_map/ppermute | solution.py:20
  71.8 38.4 %psum.36 = f32[256]{0:T(256)S(1)} all-reduce(f32[256]{0:T(256)S(1)} %multiply_reduce_fusion.3), channel_id=1, replica_groups=mesh['gx'=4,'gy'=8] {'gx','gy'}, use_global_device_ids=true, to_apply=%region_2.0 | all-reduce | flops 256 | bytes 2048 | tf_op jit(solution)/shard_map/psum | solution.py:68
  121.8 6.7 %collective-permute-start.6 = (f32[514,1]{1,0:T(8,128)S(1)}, f32[514,1]{1,0:T(8,128)S(1)}, u32[]{:S(2)}, u32[]{:S(2)}) collective-permute-start(f32[514,1]{1,0:T(8,128)S(1)} %get-tuple-element.14), channel_id=1, source_target_pairs={{0,1},{1,2},{2,3},{3,4},{4,5},{5,6},{6,7},{8,9},{9,10},{10,11},{11... | collective-permute-start | bytes 6176 | tf_op jit(solution)/shard_map/ppermute | solution.py:18
  131.9 4.5 %collective-permute-done.7 = f32[514,1]{1,0:T(8,128)S(1)} collective-permute-done((f32[514,1]{1,0:T(8,128)S(1)}, f32[514,1]{1,0:T(8,128)S(1)}, u32[]{:S(2)}, u32[]{:S(2)}) %collective-permute-start.7) | collective-permute-done | bytes 2088 | tf_op jit(solution)/shard_map/ppermute | solution.py:20
  143.2 37.7 %psum.37 = f32[256]{0:T(256)S(1)} all-reduce(f32[256]{0:T(256)S(1)} %multiply_reduce_fusion.2), channel_id=1, replica_groups=mesh['gx'=4,'gy'=8] {'gx','gy'}, use_global_device_ids=true, to_apply=%region_4.0 | all-reduce | flops 256 | bytes 2048 | tf_op jit(solution)/shard_map/psum | solution.py:68
  183.1 2.9 subtract_divide_fusion.1
  186.0 3.1 collective-permute-start.8
  190.5 3.0 collective-permute-done.9
  193.6 6.7 %collective-permute-start.10 = (f32[514,1]{1,0:T(8,128)S(1)}, f32[514,1]{1,0:T(8,128)S(1)}, u32[]{:S(2)}, u32[]{:S(2)}) collective-permute-start(f32[514,1]{1,0:T(8,128)S(1)} %get-tuple-element.12), channel_id=1, source_target_pairs={{0,1},{1,2},{2,3},{3,4},{4,5},{5,6},{6,7},{8,9},{9,10},{10,11},{11... | collective-permute-start | bytes 6176 | tf_op jit(solution)/shard_map/ppermute | solution.py:18
  203.7 4.5 %collective-permute-done.11 = f32[514,1]{1,0:T(8,128)S(1)} collective-permute-done((f32[514,1]{1,0:T(8,128)S(1)}, f32[514,1]{1,0:T(8,128)S(1)}, u32[]{:S(2)}, u32[]{:S(2)}) %collective-permute-start.11) | collective-permute-done | bytes 2088 | tf_op jit(solution)/shard_map/ppermute | solution.py:20
  215.0 37.8 %psum.38 = f32[256]{0:T(256)S(1)} all-reduce(f32[256]{0:T(256)S(1)} %multiply_reduce_fusion.1), channel_id=1, replica_groups=mesh['gx'=4,'gy'=8] {'gx','gy'}, use_global_device_ids=true, to_apply=%region_6.0 | all-reduce | flops 256 | bytes 2048 | tf_op jit(solution)/shard_map/psum | solution.py:68
  254.9 3.9 %subtract_divide_fusion = f32[512,512]{1,0:T(8,128)S(1)} fusion(f32[512,512]{1,0:T(8,128)} %copy-done.2, f32[512,512]{1,0:T(8,128)S(1)} %subtract_divide_fusion.2, f32[512,512]{1,0:T(8,128)} %copy-done.16, f32[]{:T(128)} %sqrt.18, f32[]{:T(128)} %bitcast.31, f32[]{:T(128)} %bitcast.30, f32[]{:T(128)} %bitcast.29, f32[512,512]{1,0:T(8,128)S(1)} %copy-done.1, ...), kind=kLoop, calls=%fused_computation.92 | loop fusion | flops 2097152 | bytes 5242900 | tf_op jit(solution)/shard_map/div | solution.py:91
  258.9 3.0 collective-permute-start.12
  263.2 3.0 collective-permute-done.13
  266.4 6.7 %collective-permute-start.14 = (f32[514,1]{1,0:T(8,128)S(1)}, f32[514,1]{1,0:T(8,128)S(1)}, u32[]{:S(2)}, u32[]{:S(2)}) collective-permute-start(f32[514,1]{1,0:T(8,128)S(1)} %get-tuple-element.10), channel_id=1, source_target_pairs={{0,1},{1,2},{2,3},{3,4},{4,5},{5,6},{6,7},{8,9},{9,10},{10,11},{11... | collective-permute-start | bytes 6176 | tf_op jit(solution)/shard_map/ppermute | solution.py:18
  276.4 4.5 %collective-permute-done.15 = f32[514,1]{1,0:T(8,128)S(1)} collective-permute-done((f32[514,1]{1,0:T(8,128)S(1)}, f32[514,1]{1,0:T(8,128)S(1)}, u32[]{:S(2)}, u32[]{:S(2)}) %collective-permute-start.15) | collective-permute-done | bytes 2088 | tf_op jit(solution)/shard_map/ppermute | solution.py:20
  286.6 37.8 %psum.39 = f32[256]{0:T(256)S(1)} all-reduce(f32[256]{0:T(256)S(1)} %multiply_reduce_fusion), channel_id=1, replica_groups=mesh['gx'=4,'gy'=8] {'gx','gy'}, use_global_device_ids=true, to_apply=%region_8.0 | all-reduce | flops 256 | bytes 2048 | tf_op jit(solution)/shard_map/psum | solution.py:68
  351.1 3.0 collective-permute-done.17
  354.3 6.7 %collective-permute-start.18 = (f32[514,1]{1,0:T(8,128)S(1)}, f32[514,1]{1,0:T(8,128)S(1)}, u32[]{:S(2)}, u32[]{:S(2)}) collective-permute-start(f32[514,1]{1,0:T(8,128)S(1)} %get-tuple-element.8), channel_id=1, source_target_pairs={{0,1},{1,2},{2,3},{3,4},{4,5},{5,6},{6,7},{8,9},{9,10},{10,11},{11... | collective-permute-start | bytes 6176 | tf_op jit(solution)/shard_map/ppermute | solution.py:18
  364.3 4.5 %collective-permute-done.19 = f32[514,1]{1,0:T(8,128)S(1)} collective-permute-done((f32[514,1]{1,0:T(8,128)S(1)}, f32[514,1]{1,0:T(8,128)S(1)}, u32[]{:S(2)}, u32[]{:S(2)}) %collective-permute-start.19) | collective-permute-done | bytes 2088 | tf_op jit(solution)/shard_map/ppermute | solution.py:20
  (127 shorter events, 74.7 us)
Async XLA Ops:
  4.0 42.2 %copy-start.1 = (f32[512,512]{1,0:T(8,128)S(1)}, f32[512,512]{1,0:T(8,128)}, u32[]{:S(2)}) copy-start(f32[512,512]{1,0:T(8,128)} %param.5) | copy-start | bytes 3145732
  46.3 4.6 %collective-permute-start = (f32[1,512]{1,0:T(1,128)S(1)}, f32[1,512]{1,0:T(1,128)S(1)}, u32[]{:S(2)}, u32[]{:S(2)}) collective-permute-start(f32[1,512]{1,0:T(1,128)S(1)} %get-tuple-element.26), channel_id=1, source_target_pairs={{0,8},{8,16},{16,24},{1,9},{9,17},{17,25},{2,10},{10,18},{18,26},{... | collective-permute-start | bytes 6152 | tf_op jit(solution)/shard_map/ppermute | solution.py:18
  49.6 4.3 %collective-permute-start.1 = (f32[1,512]{1,0:T(1,128)S(1)}, f32[1,512]{1,0:T(1,128)S(1)}, u32[]{:S(2)}, u32[]{:S(2)}) collective-permute-start(f32[1,512]{1,0:T(1,128)S(1)} %get-tuple-element.27), channel_id=1, source_target_pairs={{8,0},{16,8},{24,16},{9,1},{17,9},{25,17},{10,2},{18,10},{26,18},{... | collective-permute-start | bytes 6152 | tf_op jit(solution)/shard_map/ppermute | solution.py:20
  54.1 10.1 %collective-permute-start.2 = (f32[514,1]{1,0:T(8,128)S(1)}, f32[514,1]{1,0:T(8,128)S(1)}, u32[]{:S(2)}, u32[]{:S(2)}) collective-permute-start(f32[514,1]{1,0:T(8,128)S(1)} %get-tuple-element.16), channel_id=1, source_target_pairs={{0,1},{1,2},{2,3},{3,4},{4,5},{5,6},{6,7},{8,9},{9,10},{10,11},{11... | collective-permute-start | bytes 6176 | tf_op jit(solution)/shard_map/ppermute | solution.py:18
  60.8 7.8 %collective-permute-start.3 = (f32[514,1]{1,0:T(8,128)S(1)}, f32[514,1]{1,0:T(8,128)S(1)}, u32[]{:S(2)}, u32[]{:S(2)}) collective-permute-start(f32[514,1]{1,0:T(8,128)S(1)} %get-tuple-element.17), channel_id=1, source_target_pairs={{1,0},{2,1},{3,2},{4,3},{5,4},{6,5},{7,6},{9,8},{10,9},{11,10},{12... | collective-permute-start | bytes 6176 | tf_op jit(solution)/shard_map/ppermute | solution.py:20
  115.0 4.4 %collective-permute-start.4 = (f32[1,512]{1,0:T(1,128)S(1)}, f32[1,512]{1,0:T(1,128)S(1)}, u32[]{:S(2)}, u32[]{:S(2)}) collective-permute-start(f32[1,512]{1,0:T(1,128)S(1)} %get-tuple-element.24), channel_id=1, source_target_pairs={{0,8},{8,16},{16,24},{1,9},{9,17},{17,25},{2,10},{10,18},{18,26},{... | collective-permute-start | bytes 6152 | tf_op jit(solution)/shard_map/ppermute | solution.py:18
  117.4 4.3 %collective-permute-start.5 = (f32[1,512]{1,0:T(1,128)S(1)}, f32[1,512]{1,0:T(1,128)S(1)}, u32[]{:S(2)}, u32[]{:S(2)}) collective-permute-start(f32[1,512]{1,0:T(1,128)S(1)} %get-tuple-element.25), channel_id=1, source_target_pairs={{8,0},{16,8},{24,16},{9,1},{17,9},{25,17},{10,2},{18,10},{26,18},{... | collective-permute-start | bytes 6152 | tf_op jit(solution)/shard_map/ppermute | solution.py:20
  121.8 10.1 %collective-permute-start.6 = (f32[514,1]{1,0:T(8,128)S(1)}, f32[514,1]{1,0:T(8,128)S(1)}, u32[]{:S(2)}, u32[]{:S(2)}) collective-permute-start(f32[514,1]{1,0:T(8,128)S(1)} %get-tuple-element.14), channel_id=1, source_target_pairs={{0,1},{1,2},{2,3},{3,4},{4,5},{5,6},{6,7},{8,9},{9,10},{10,11},{11... | collective-permute-start | bytes 6176 | tf_op jit(solution)/shard_map/ppermute | solution.py:18
  128.6 7.8 %collective-permute-start.7 = (f32[514,1]{1,0:T(8,128)S(1)}, f32[514,1]{1,0:T(8,128)S(1)}, u32[]{:S(2)}, u32[]{:S(2)}) collective-permute-start(f32[514,1]{1,0:T(8,128)S(1)} %get-tuple-element.15), channel_id=1, source_target_pairs={{1,0},{2,1},{3,2},{4,3},{5,4},{6,5},{7,6},{9,8},{10,9},{11,10},{12... | collective-permute-start | bytes 6176 | tf_op jit(solution)/shard_map/ppermute | solution.py:20
  183.1 25.1 %copy-start.10 = (f32[512,512]{1,0:T(8,128)S(1)}, f32[512,512]{1,0:T(8,128)}, u32[]{:S(2)}) copy-start(f32[512,512]{1,0:T(8,128)} %param.6) | copy-start | bytes 3145732
  186.0 4.4 %collective-permute-start.8 = (f32[1,512]{1,0:T(1,128)S(1)}, f32[1,512]{1,0:T(1,128)S(1)}, u32[]{:S(2)}, u32[]{:S(2)}) collective-permute-start(f32[1,512]{1,0:T(1,128)S(1)} %get-tuple-element.22), channel_id=1, source_target_pairs={{0,8},{8,16},{16,24},{1,9},{9,17},{17,25},{2,10},{10,18},{18,26},{... | collective-permute-start | bytes 6152 | tf_op jit(solution)/shard_map/ppermute | solution.py:18
  189.1 4.3 %collective-permute-start.9 = (f32[1,512]{1,0:T(1,128)S(1)}, f32[1,512]{1,0:T(1,128)S(1)}, u32[]{:S(2)}, u32[]{:S(2)}) collective-permute-start(f32[1,512]{1,0:T(1,128)S(1)} %get-tuple-element.23), channel_id=1, source_target_pairs={{8,0},{16,8},{24,16},{9,1},{17,9},{25,17},{10,2},{18,10},{26,18},{... | collective-permute-start | bytes 6152 | tf_op jit(solution)/shard_map/ppermute | solution.py:20
  193.6 10.1 %collective-permute-start.10 = (f32[514,1]{1,0:T(8,128)S(1)}, f32[514,1]{1,0:T(8,128)S(1)}, u32[]{:S(2)}, u32[]{:S(2)}) collective-permute-start(f32[514,1]{1,0:T(8,128)S(1)} %get-tuple-element.12), channel_id=1, source_target_pairs={{0,1},{1,2},{2,3},{3,4},{4,5},{5,6},{6,7},{8,9},{9,10},{10,11},{11... | collective-permute-start | bytes 6176 | tf_op jit(solution)/shard_map/ppermute | solution.py:18
  200.3 7.8 %collective-permute-start.11 = (f32[514,1]{1,0:T(8,128)S(1)}, f32[514,1]{1,0:T(8,128)S(1)}, u32[]{:S(2)}, u32[]{:S(2)}) collective-permute-start(f32[514,1]{1,0:T(8,128)S(1)} %get-tuple-element.13), channel_id=1, source_target_pairs={{1,0},{2,1},{3,2},{4,3},{5,4},{6,5},{7,6},{9,8},{10,9},{11,10},{12... | collective-permute-start | bytes 6176 | tf_op jit(solution)/shard_map/ppermute | solution.py:20
  254.9 26.0 %copy-start.11 = (f32[512,512]{1,0:T(8,128)S(1)}, f32[512,512]{1,0:T(8,128)}, u32[]{:S(2)}) copy-start(f32[512,512]{1,0:T(8,128)} %param.6) | copy-start | bytes 3145732
  258.9 4.3 %collective-permute-start.12 = (f32[1,512]{1,0:T(1,128)S(1)}, f32[1,512]{1,0:T(1,128)S(1)}, u32[]{:S(2)}, u32[]{:S(2)}) collective-permute-start(f32[1,512]{1,0:T(1,128)S(1)} %get-tuple-element.20), channel_id=1, source_target_pairs={{0,8},{8,16},{16,24},{1,9},{9,17},{17,25},{2,10},{10,18},{18,26},{... | collective-permute-start | bytes 6152 | tf_op jit(solution)/shard_map/ppermute | solution.py:18
  261.9 4.3 %collective-permute-start.13 = (f32[1,512]{1,0:T(1,128)S(1)}, f32[1,512]{1,0:T(1,128)S(1)}, u32[]{:S(2)}, u32[]{:S(2)}) collective-permute-start(f32[1,512]{1,0:T(1,128)S(1)} %get-tuple-element.21), channel_id=1, source_target_pairs={{8,0},{16,8},{24,16},{9,1},{17,9},{25,17},{10,2},{18,10},{26,18},{... | collective-permute-start | bytes 6152 | tf_op jit(solution)/shard_map/ppermute | solution.py:20
  266.4 10.1 %collective-permute-start.14 = (f32[514,1]{1,0:T(8,128)S(1)}, f32[514,1]{1,0:T(8,128)S(1)}, u32[]{:S(2)}, u32[]{:S(2)}) collective-permute-start(f32[514,1]{1,0:T(8,128)S(1)} %get-tuple-element.10), channel_id=1, source_target_pairs={{0,1},{1,2},{2,3},{3,4},{4,5},{5,6},{6,7},{8,9},{9,10},{10,11},{11... | collective-permute-start | bytes 6176 | tf_op jit(solution)/shard_map/ppermute | solution.py:18
  273.1 7.8 %collective-permute-start.15 = (f32[514,1]{1,0:T(8,128)S(1)}, f32[514,1]{1,0:T(8,128)S(1)}, u32[]{:S(2)}, u32[]{:S(2)}) collective-permute-start(f32[514,1]{1,0:T(8,128)S(1)} %get-tuple-element.11), channel_id=1, source_target_pairs={{1,0},{2,1},{3,2},{4,3},{5,4},{6,5},{7,6},{9,8},{10,9},{11,10},{12... | collective-permute-start | bytes 6176 | tf_op jit(solution)/shard_map/ppermute | solution.py:20
  344.7 24.1 %copy-start.12 = (f32[512,512]{1,0:T(8,128)S(1)}, f32[512,512]{1,0:T(8,128)}, u32[]{:S(2)}) copy-start(f32[512,512]{1,0:T(8,128)} %param.6) | copy-start | bytes 3145732
  346.9 4.2 %collective-permute-start.16 = (f32[1,512]{1,0:T(1,128)S(1)}, f32[1,512]{1,0:T(1,128)S(1)}, u32[]{:S(2)}, u32[]{:S(2)}) collective-permute-start(f32[1,512]{1,0:T(1,128)S(1)} %get-tuple-element.18), channel_id=1, source_target_pairs={{0,8},{8,16},{16,24},{1,9},{9,17},{17,25},{2,10},{10,18},{18,26},{... | collective-permute-start | bytes 6152 | tf_op jit(solution)/shard_map/ppermute | solution.py:18
  349.8 4.3 %collective-permute-start.17 = (f32[1,512]{1,0:T(1,128)S(1)}, f32[1,512]{1,0:T(1,128)S(1)}, u32[]{:S(2)}, u32[]{:S(2)}) collective-permute-start(f32[1,512]{1,0:T(1,128)S(1)} %get-tuple-element.19), channel_id=1, source_target_pairs={{8,0},{16,8},{24,16},{9,1},{17,9},{25,17},{10,2},{18,10},{26,18},{... | collective-permute-start | bytes 6152 | tf_op jit(solution)/shard_map/ppermute | solution.py:20
  354.3 10.1 %collective-permute-start.18 = (f32[514,1]{1,0:T(8,128)S(1)}, f32[514,1]{1,0:T(8,128)S(1)}, u32[]{:S(2)}, u32[]{:S(2)}) collective-permute-start(f32[514,1]{1,0:T(8,128)S(1)} %get-tuple-element.8), channel_id=1, source_target_pairs={{0,1},{1,2},{2,3},{3,4},{4,5},{5,6},{6,7},{8,9},{9,10},{10,11},{11... | collective-permute-start | bytes 6176 | tf_op jit(solution)/shard_map/ppermute | solution.py:18
  361.0 7.8 %collective-permute-start.19 = (f32[514,1]{1,0:T(8,128)S(1)}, f32[514,1]{1,0:T(8,128)S(1)}, u32[]{:S(2)}, u32[]{:S(2)}) collective-permute-start(f32[514,1]{1,0:T(8,128)S(1)} %get-tuple-element.9), channel_id=1, source_target_pairs={{1,0},{2,1},{3,2},{4,3},{5,4},{6,5},{7,6},{9,8},{10,9},{11,10},{12... | collective-permute-start | bytes 6176 | tf_op jit(solution)/shard_map/ppermute | solution.py:20
  (15 other events, 231.2 us)
where the time goes:
time: 372 us; the launch traced here: 371 us
  blocking collectives  192 us (52%)
  starting transfers between devices  64.4 us (17%)
  waiting for transfers between devices  42.7 us (11%)
  other arithmetic  28.1 us (8%)
  between operations  19.8 us (5%)
  local copies, waits for them, and re-layouts  13.1 us (4%)
  matrix products  10.4 us (3%)
    psum x5, blocking collectives, sketch(): return lax.psum(partial_value, ('gx', 'gy'))  192 us
    ppermute x10, starting transfers between devices, padded_2(): lax.ppermute(tail, axis, [(i, (i + 1) % count) for i in range(ends)])  48.2 us
    ppermute x10, waiting for transfers between devices, padded_2(): lax.ppermute(head, axis, [((i + 1) % count, i) for i in range(ends)])  36.7 us
    ppermute x10, starting transfers between devices, padded_2(): lax.ppermute(head, axis, [((i + 1) % count, i) for i in range(ends)])  16.2 us
    unnamed x43, local copies, waits for them, and re-layouts  10.5 us
    dot_general x5, matrix products, sketch(): product = jnp.dot(field, sketch_cols.T, precision=lax.Precision.HIGHEST)  9.45 us
    div x3, other arithmetic, body(): basis_vectors.append(remainder / new_norm)  9.05 us
  transfers between devices with their start and end apart: 20, of which 15 were waited for; matrix products, arithmetic and copies ran while one was open for 0% of the time, Pallas kernels for 0%

commit v1 on v0

--- a/solution.py
+++ b/solution.py
@@ -65,7 +65,7 @@
         partial_value = jnp.einsum(
             "ki,ik->k", sketch_rows, product, precision=lax.Precision.HIGHEST
         )
-        return lax.psum(partial_value, ("gx", "gy"))
+        return jnp.sum(lax.all_gather(partial_value, ("gx", "gy")), axis=0)
 
     first_sketch = sketch(right_side)
     beta_norm = jnp.sqrt(jnp.sum(first_sketch * first_sketch))

time: 372 us -> 341 us (0.917)
  starting transfers between devices: 64.4 us -> 36.2 us
    psum x5 -> x0, blocking collectives: 192 us -> none  [sketch(): return lax.psum(partial_value, ('gx', 'gy'))]
    all_gather x0 -> x5, blocking collectives: none -> 192 us  [sketch(): return jnp.sum(lax.all_gather(partial_value, ('gx', 'gy')), axis=0)]
    ppermute x10, starting transfers between devices: 48.2 us -> 16.7 us  [padded_2(): lax.ppermute(tail, axis, [(i, (i + 1) % count) for i in range(ends)])]
where the time goes in v1:
time: 341 us; the launch traced here: 339 us
  blocking collectives  192 us (56%)
  waiting for transfers between devices  39.9 us (12%)
  starting transfers between devices  36.2 us (11%)
  other arithmetic  27.8 us (8%)
  between operations  19.8 us (6%)
  local copies, waits for them, and re-layouts  13.2 us (4%)
  matrix products  10.4 us (3%)
    all_gather x5, blocking collectives, sketch(): return jnp.sum(lax.all_gather(partial_value, ('gx', 'gy')), axis=0)  192 us
    ppermute x10, waiting for transfers between devices, padded_2(): lax.ppermute(head, axis, [((i + 1) % count, i) for i in range(ends)])  37 us
    ppermute x10, starting transfers between devices, padded_2(): lax.ppermute(head, axis, [((i + 1) % count, i) for i in range(ends)])  19.5 us
    ppermute x10, starting transfers between devices, padded_2(): lax.ppermute(tail, axis, [(i, (i + 1) % count) for i in range(ends)])  16.7 us
    unnamed x43, local copies, waits for them, and re-layouts  10.5 us
    dot_general x5, matrix products, sketch(): product = jnp.dot(field, sketch_cols.T, precision=lax.Precision.HIGHEST)  9.44 us
    div x3, other arithmetic, body(): basis_vectors.append(remainder / new_norm)  9.04 us
  transfers between devices with their start and end apart: 20, of which 15 were waited for; matrix products, arithmetic and copies ran while one was open for 0% of the time, Pallas kernels for 0%

profile of v1, /device:TPU:1, one launch (start us, length us, event | category | flops | bytes accessed | tf_op | source)
XLA Modules:
  0.0 339.3 jit_solution(9830431276913863019)
XLA Ops:
  1.7 2.3 convolution_bitcast_fusion.4
  4.3 43.2 %all-gather.5 = f32[32,1,256]{2,1,0:T(1,128)S(1)} all-gather(f32[1,1,256]{2,1,0:T(1,128)S(1)} %bitcast.104), channel_id=2, replica_groups=mesh['gx'=4,'gy'=8] {'gx','gy'}, dimensions={0}, use_global_device_ids=true | all-gather | bytes 33792 | tf_op jit(solution)/shard_map/all_gather | solution.py:68
  51.8 3.0 collective-permute-done.1
  56.9 2.6 collective-permute-start.3
  60.2 4.4 %collective-permute-done.3 = f32[514,1]{1,0:T(8,128)S(1)} collective-permute-done((f32[514,1]{1,0:T(8,128)S(1)}, f32[514,1]{1,0:T(8,128)S(1)}, u32[]{:S(2)}, u32[]{:S(2)}) %collective-permute-start.3) | collective-permute-done | bytes 2088 | tf_op jit(solution)/shard_map/ppermute | solution.py:20
  67.8 37.2 %all-gather.6 = f32[32,1,256]{2,1,0:T(1,128)S(1)} all-gather(f32[1,1,256]{2,1,0:T(1,128)S(1)} %bitcast.105), channel_id=3, replica_groups=mesh['gx'=4,'gy'=8] {'gx','gy'}, dimensions={0}, use_global_device_ids=true | all-gather | bytes 33792 | tf_op jit(solution)/shard_map/all_gather | solution.py:68
  112.4 3.0 collective-permute-done.5
  117.5 2.6 collective-permute-start.7
  120.8 4.4 %collective-permute-done.7 = f32[514,1]{1,0:T(8,128)S(1)} collective-permute-done((f32[514,1]{1,0:T(8,128)S(1)}, f32[514,1]{1,0:T(8,128)S(1)}, u32[]{:S(2)}, u32[]{:S(2)}) %collective-permute-start.7) | collective-permute-done | bytes 2088 | tf_op jit(solution)/shard_map/ppermute | solution.py:20
  132.1 37.2 %all-gather.7 = f32[32,1,256]{2,1,0:T(1,128)S(1)} all-gather(f32[1,1,256]{2,1,0:T(1,128)S(1)} %bitcast.106), channel_id=4, replica_groups=mesh['gx'=4,'gy'=8] {'gx','gy'}, dimensions={0}, use_global_device_ids=true | all-gather | bytes 33792 | tf_op jit(solution)/shard_map/all_gather | solution.py:68
  171.5 2.9 subtract_divide_fusion.1
  177.2 3.0 collective-permute-done.9
  182.2 2.6 collective-permute-start.11
  185.6 4.4 %collective-permute-done.11 = f32[514,1]{1,0:T(8,128)S(1)} collective-permute-done((f32[514,1]{1,0:T(8,128)S(1)}, f32[514,1]{1,0:T(8,128)S(1)}, u32[]{:S(2)}, u32[]{:S(2)}) %collective-permute-start.11) | collective-permute-done | bytes 2088 | tf_op jit(solution)/shard_map/ppermute | solution.py:20
  196.8 37.3 %all-gather.8 = f32[32,1,256]{2,1,0:T(1,128)S(1)} all-gather(f32[1,1,256]{2,1,0:T(1,128)S(1)} %bitcast.107), channel_id=5, replica_groups=mesh['gx'=4,'gy'=8] {'gx','gy'}, dimensions={0}, use_global_device_ids=true | all-gather | bytes 33792 | tf_op jit(solution)/shard_map/all_gather | solution.py:68
  236.5 4.0 %subtract_divide_fusion = f32[512,512]{1,0:T(8,128)S(1)} fusion(f32[512,512]{1,0:T(8,128)} %copy-done.2, f32[512,512]{1,0:T(8,128)S(1)} %subtract_divide_fusion.2, f32[512,512]{1,0:T(8,128)} %copy-done.16, f32[]{:T(128)} %sqrt.18, f32[]{:T(128)} %bitcast.35, f32[]{:T(128)} %bitcast.34, f32[]{:T(128)} %bitcast.33, f32[512,512]{1,0:T(8,128)S(1)} %copy-done.1, ...), kind=kLoop, calls=%fused_computation.92 | loop fusion | flops 2097152 | bytes 5242900 | tf_op jit(solution)/shard_map/div | solution.py:91
  243.3 3.0 collective-permute-done.13
  248.3 2.6 collective-permute-start.15
  251.7 4.4 %collective-permute-done.15 = f32[514,1]{1,0:T(8,128)S(1)} collective-permute-done((f32[514,1]{1,0:T(8,128)S(1)}, f32[514,1]{1,0:T(8,128)S(1)}, u32[]{:S(2)}, u32[]{:S(2)}) %collective-permute-start.15) | collective-permute-done | bytes 2088 | tf_op jit(solution)/shard_map/ppermute | solution.py:20
  256.1 2.5 convolution_bitcast_fusion
  261.8 37.2 %all-gather.9 = f32[32,1,256]{2,1,0:T(1,128)S(1)} all-gather(f32[1,1,256]{2,1,0:T(1,128)S(1)} %bitcast.108), channel_id=6, replica_groups=mesh['gx'=4,'gy'=8] {'gx','gy'}, dimensions={0}, use_global_device_ids=true | all-gather | bytes 33792 | tf_op jit(solution)/shard_map/all_gather | solution.py:68
  324.6 3.0 collective-permute-done.17
  329.7 2.6 collective-permute-start.19
  333.0 4.4 %collective-permute-done.19 = f32[514,1]{1,0:T(8,128)S(1)} collective-permute-done((f32[514,1]{1,0:T(8,128)S(1)}, f32[514,1]{1,0:T(8,128)S(1)}, u32[]{:S(2)}, u32[]{:S(2)}) %collective-permute-start.19) | collective-permute-done | bytes 2088 | tf_op jit(solution)/shard_map/ppermute | solution.py:20
  (131 shorter events, 65.7 us)
Async XLA Ops:
  4.0 44.9 %copy-start.1 = (f32[512,512]{1,0:T(8,128)S(1)}, f32[512,512]{1,0:T(8,128)}, u32[]{:S(2)}) copy-start(f32[512,512]{1,0:T(8,128)} %param.5) | copy-start | bytes 3145732
  49.1 2.7 collective-permute-start
  50.5 4.3 %collective-permute-start.1 = (f32[1,512]{1,0:T(1,128)S(1)}, f32[1,512]{1,0:T(1,128)S(1)}, u32[]{:S(2)}, u32[]{:S(2)}) collective-permute-start(f32[1,512]{1,0:T(1,128)S(1)} %get-tuple-element.27), channel_id=1, source_target_pairs={{8,0},{16,8},{24,16},{9,1},{17,9},{25,17},{10,2},{18,10},{26,18},{... | collective-permute-start | bytes 6152 | tf_op jit(solution)/shard_map/ppermute | solution.py:20
  55.0 5.3 %collective-permute-start.2 = (f32[514,1]{1,0:T(8,128)S(1)}, f32[514,1]{1,0:T(8,128)S(1)}, u32[]{:S(2)}, u32[]{:S(2)}) collective-permute-start(f32[514,1]{1,0:T(8,128)S(1)} %get-tuple-element.16), channel_id=1, source_target_pairs={{0,1},{1,2},{2,3},{3,4},{4,5},{5,6},{6,7},{8,9},{9,10},{10,11},{11... | collective-permute-start | bytes 6176 | tf_op jit(solution)/shard_map/ppermute | solution.py:18
  56.9 7.7 %collective-permute-start.3 = (f32[514,1]{1,0:T(8,128)S(1)}, f32[514,1]{1,0:T(8,128)S(1)}, u32[]{:S(2)}, u32[]{:S(2)}) collective-permute-start(f32[514,1]{1,0:T(8,128)S(1)} %get-tuple-element.17), channel_id=1, source_target_pairs={{1,0},{2,1},{3,2},{4,3},{5,4},{6,5},{7,6},{9,8},{10,9},{11,10},{12... | collective-permute-start | bytes 6176 | tf_op jit(solution)/shard_map/ppermute | solution.py:20
  109.6 2.7 collective-permute-start.4
  111.1 4.3 %collective-permute-start.5 = (f32[1,512]{1,0:T(1,128)S(1)}, f32[1,512]{1,0:T(1,128)S(1)}, u32[]{:S(2)}, u32[]{:S(2)}) collective-permute-start(f32[1,512]{1,0:T(1,128)S(1)} %get-tuple-element.25), channel_id=1, source_target_pairs={{8,0},{16,8},{24,16},{9,1},{17,9},{25,17},{10,2},{18,10},{26,18},{... | collective-permute-start | bytes 6152 | tf_op jit(solution)/shard_map/ppermute | solution.py:20
  115.5 5.3 %collective-permute-start.6 = (f32[514,1]{1,0:T(8,128)S(1)}, f32[514,1]{1,0:T(8,128)S(1)}, u32[]{:S(2)}, u32[]{:S(2)}) collective-permute-start(f32[514,1]{1,0:T(8,128)S(1)} %get-tuple-element.14), channel_id=1, source_target_pairs={{0,1},{1,2},{2,3},{3,4},{4,5},{5,6},{6,7},{8,9},{9,10},{10,11},{11... | collective-permute-start | bytes 6176 | tf_op jit(solution)/shard_map/ppermute | solution.py:18
  117.5 7.7 %collective-permute-start.7 = (f32[514,1]{1,0:T(8,128)S(1)}, f32[514,1]{1,0:T(8,128)S(1)}, u32[]{:S(2)}, u32[]{:S(2)}) collective-permute-start(f32[514,1]{1,0:T(8,128)S(1)} %get-tuple-element.15), channel_id=1, source_target_pairs={{1,0},{2,1},{3,2},{4,3},{5,4},{6,5},{7,6},{9,8},{10,9},{11,10},{12... | collective-permute-start | bytes 6176 | tf_op jit(solution)/shard_map/ppermute | solution.py:20
  171.5 18.5 %copy-start.10 = (f32[512,512]{1,0:T(8,128)S(1)}, f32[512,512]{1,0:T(8,128)}, u32[]{:S(2)}) copy-start(f32[512,512]{1,0:T(8,128)} %param.6) | copy-start | bytes 3145732
  174.4 2.7 collective-permute-start.8
  175.8 4.3 %collective-permute-start.9 = (f32[1,512]{1,0:T(1,128)S(1)}, f32[1,512]{1,0:T(1,128)S(1)}, u32[]{:S(2)}, u32[]{:S(2)}) collective-permute-start(f32[1,512]{1,0:T(1,128)S(1)} %get-tuple-element.23), channel_id=1, source_target_pairs={{8,0},{16,8},{24,16},{9,1},{17,9},{25,17},{10,2},{18,10},{26,18},{... | collective-permute-start | bytes 6152 | tf_op jit(solution)/shard_map/ppermute | solution.py:20
  180.3 5.3 %collective-permute-start.10 = (f32[514,1]{1,0:T(8,128)S(1)}, f32[514,1]{1,0:T(8,128)S(1)}, u32[]{:S(2)}, u32[]{:S(2)}) collective-permute-start(f32[514,1]{1,0:T(8,128)S(1)} %get-tuple-element.12), channel_id=1, source_target_pairs={{0,1},{1,2},{2,3},{3,4},{4,5},{5,6},{6,7},{8,9},{9,10},{10,11},{11... | collective-permute-start | bytes 6176 | tf_op jit(solution)/shard_map/ppermute | solution.py:18
  182.2 7.7 %collective-permute-start.11 = (f32[514,1]{1,0:T(8,128)S(1)}, f32[514,1]{1,0:T(8,128)S(1)}, u32[]{:S(2)}, u32[]{:S(2)}) collective-permute-start(f32[514,1]{1,0:T(8,128)S(1)} %get-tuple-element.13), channel_id=1, source_target_pairs={{1,0},{2,1},{3,2},{4,3},{5,4},{6,5},{7,6},{9,8},{10,9},{11,10},{12... | collective-permute-start | bytes 6176 | tf_op jit(solution)/shard_map/ppermute | solution.py:20
  236.5 19.6 %copy-start.11 = (f32[512,512]{1,0:T(8,128)S(1)}, f32[512,512]{1,0:T(8,128)}, u32[]{:S(2)}) copy-start(f32[512,512]{1,0:T(8,128)} %param.6) | copy-start | bytes 3145732
  240.5 2.7 collective-permute-start.12
  241.9 4.3 %collective-permute-start.13 = (f32[1,512]{1,0:T(1,128)S(1)}, f32[1,512]{1,0:T(1,128)S(1)}, u32[]{:S(2)}, u32[]{:S(2)}) collective-permute-start(f32[1,512]{1,0:T(1,128)S(1)} %get-tuple-element.21), channel_id=1, source_target_pairs={{8,0},{16,8},{24,16},{9,1},{17,9},{25,17},{10,2},{18,10},{26,18},{... | collective-permute-start | bytes 6152 | tf_op jit(solution)/shard_map/ppermute | solution.py:20
  246.4 5.3 %collective-permute-start.14 = (f32[514,1]{1,0:T(8,128)S(1)}, f32[514,1]{1,0:T(8,128)S(1)}, u32[]{:S(2)}, u32[]{:S(2)}) collective-permute-start(f32[514,1]{1,0:T(8,128)S(1)} %get-tuple-element.10), channel_id=1, source_target_pairs={{0,1},{1,2},{2,3},{3,4},{4,5},{5,6},{6,7},{8,9},{9,10},{10,11},{11... | collective-permute-start | bytes 6176 | tf_op jit(solution)/shard_map/ppermute | solution.py:18
  248.3 7.7 %collective-permute-start.15 = (f32[514,1]{1,0:T(8,128)S(1)}, f32[514,1]{1,0:T(8,128)S(1)}, u32[]{:S(2)}, u32[]{:S(2)}) collective-permute-start(f32[514,1]{1,0:T(8,128)S(1)} %get-tuple-element.11), channel_id=1, source_target_pairs={{1,0},{2,1},{3,2},{4,3},{5,4},{6,5},{7,6},{9,8},{10,9},{11,10},{12... | collective-permute-start | bytes 6176 | tf_op jit(solution)/shard_map/ppermute | solution.py:20
  319.6 17.8 %copy-start.12 = (f32[512,512]{1,0:T(8,128)S(1)}, f32[512,512]{1,0:T(8,128)}, u32[]{:S(2)}) copy-start(f32[512,512]{1,0:T(8,128)} %param.6) | copy-start | bytes 3145732
  321.8 2.7 collective-permute-start.16
  323.3 4.3 %collective-permute-start.17 = (f32[1,512]{1,0:T(1,128)S(1)}, f32[1,512]{1,0:T(1,128)S(1)}, u32[]{:S(2)}, u32[]{:S(2)}) collective-permute-start(f32[1,512]{1,0:T(1,128)S(1)} %get-tuple-element.19), channel_id=1, source_target_pairs={{8,0},{16,8},{24,16},{9,1},{17,9},{25,17},{10,2},{18,10},{26,18},{... | collective-permute-start | bytes 6152 | tf_op jit(solution)/shard_map/ppermute | solution.py:20
  327.7 5.3 %collective-permute-start.18 = (f32[514,1]{1,0:T(8,128)S(1)}, f32[514,1]{1,0:T(8,128)S(1)}, u32[]{:S(2)}, u32[]{:S(2)}) collective-permute-start(f32[514,1]{1,0:T(8,128)S(1)} %get-tuple-element.8), channel_id=1, source_target_pairs={{0,1},{1,2},{2,3},{3,4},{4,5},{5,6},{6,7},{8,9},{9,10},{10,11},{11... | collective-permute-start | bytes 6176 | tf_op jit(solution)/shard_map/ppermute | solution.py:18
  329.7 7.7 %collective-permute-start.19 = (f32[514,1]{1,0:T(8,128)S(1)}, f32[514,1]{1,0:T(8,128)S(1)}, u32[]{:S(2)}, u32[]{:S(2)}) collective-permute-start(f32[514,1]{1,0:T(8,128)S(1)} %get-tuple-element.9), channel_id=1, source_target_pairs={{1,0},{2,1},{3,2},{4,3},{5,4},{6,5},{7,6},{9,8},{10,9},{11,10},{12... | collective-permute-start | bytes 6176 | tf_op jit(solution)/shard_map/ppermute | solution.py:20
  (15 other events, 167.5 us)
